TPU v7x, 32 devices: a whole 2x2x4 slice. The times are simulated.
32 devices in a mesh: rep: 2 (over x), grp: 2 (over core), ep: 8 (over z, y).
Axes of the slice: x: 2, y: 2, z: 4, core: 2. Of those that a mesh axis runs over, the one named last changes fastest.
Arguments:
- tokens: bfloat16 [4096, 2048], P(('rep', 'grp', 'ep')), parts along dimension 0, may hold values from -6 to 6
- routes: int32 [4096, 8], P(('rep', 'grp', 'ep')), parts along dimension 0, may hold values from 0 to 15, all different within a row; in each aligned block of 128 rows (0 to 127, 128 to 255, ...) at most 96 rows name the same one
- gates: float32 [4096, 8], P(('rep', 'grp', 'ep')), parts along dimension 0, may hold values from 0.1 to 1
- w_gate: bfloat16 [16, 2048, 768], P(('grp', 'ep')), may hold values from -0.125 to 0.125
- w_up: bfloat16 [16, 2048, 768], P(('grp', 'ep')), may hold values from -0.125 to 0.125
- w_down: bfloat16 [16, 768, 2048], P(('grp', 'ep')), may hold values from -0.21875 to 0.21875
Outputs:
- mixed: bfloat16 [4096, 2048], P(('rep', 'grp', 'ep')), parts along dimension 0
There are 2 independent parts, one for each index of `rep`. A program takes and returns all parts, laid end to end along the dimension named above; an argument that names none is the same for every part. Nothing has to cross between parts.
Inputs may be any that keep to these rules, and one draw needn't show every extreme that they name: `routes`: each row names 8 different experts; within the rows of one device no expert is named by more than 96 rows, a bound that some block reaches.
All inputs are finite; a program needn't handle non-finite values.
Results may differ from a plain program's by a relative error of at most 0.0057.
Values may be sent and summed in bfloat16 or wider, within the bound.
A program may use at most 128 MiB of HBM per device.

v0:
```python
import jax
import jax.numpy as jnp
from jax import lax
from jax.sharding import PartitionSpec as P


def expert_rows(rows, w_gate, w_up, w_down):
    gate_act = jnp.dot(rows, w_gate[0], preferred_element_type=jnp.float32)
    up_act = jnp.dot(rows, w_up[0], preferred_element_type=jnp.float32)
    hidden = (jax.nn.silu(gate_act) * up_act).astype(jnp.bfloat16)
    return jnp.dot(hidden, w_down[0], preferred_element_type=jnp.float32).astype(jnp.bfloat16)


def local(tokens, routes, gates, w_gate, w_up, w_down):
    tok_rows, width = tokens.shape
    top = routes.shape[1]
    groups = lax.axis_size("grp")
    members = lax.axis_size("ep")
    experts = groups * members
    capacity = tok_rows * top * 3 // (2 * experts)
    flat_ids = routes.reshape(-1)
    onehot = (flat_ids[:, None] == jnp.arange(experts, dtype=jnp.int32)[None, :]).astype(jnp.int32)
    ranks = jnp.cumsum(onehot, axis=0) - 1
    slot = jnp.sum(ranks * onehot, axis=1)
    position = flat_ids * capacity + slot
    token_idx = jnp.arange(tok_rows * top, dtype=jnp.int32) // top
    send = jnp.zeros((experts * capacity, width), jnp.bfloat16).at[position].set(tokens[token_idx])
    sectioned = send.reshape(groups, members, capacity, width)
    arrived = lax.all_to_all(
        lax.all_to_all(sectioned, "grp", split_axis=0, concat_axis=0, tiled=True),
        "ep",
        split_axis=1,
        concat_axis=1,
        tiled=True,
    )
    results = expert_rows(arrived.reshape(-1, width), w_gate, w_up, w_down)
    results = results.reshape(groups, members, capacity, width)
    back = lax.all_to_all(
        lax.all_to_all(results, "grp", split_axis=0, concat_axis=0, tiled=True),
        "ep",
        split_axis=1,
        concat_axis=1,
        tiled=True,
    )
    picked = back.reshape(experts * capacity, width)[position].astype(jnp.float32)
    picked = picked.reshape(tok_rows, top, width)
    mixed = jnp.sum(picked * gates[:, :, None], axis=1)
    return mixed.astype(jnp.bfloat16)


def solution(mesh):
    return jax.shard_map(
        local,
        mesh=mesh,
        in_specs=(
            P(("rep", "grp", "ep"), None),
            P(("rep", "grp", "ep"), None),
            P(("rep", "grp", "ep"), None),
            P(("grp", "ep"), None, None),
            P(("grp", "ep"), None, None),
            P(("grp", "ep"), None, None),
        ),
        out_specs=P(("rep", "grp", "ep"), None),
        check_vma=False,
    )
```

profile of v0, /device:TPU:0, one launch (start us, length us, event | category | flops | bytes accessed | tf_op | source)
XLA Modules:
  0.0 388.4 jit_solution(647400125699474059)
XLA Ops:
  0.0 0.0 copy-start
  0.0 0.9 copy.35
  0.9 0.1 eq.29
  1.0 0.1 eq.25
  1.1 0.7 broadcast_multiply_fusion
  1.8 4.5 %reduce-window.6 = s32[16,8,128]{2,1,0:T(8,128)S(1)} reduce-window(s32[16,8,128]{2,1,0:T(8,128)S(1)} %fusion.10, s32[]{:T(128)} %constant.30.clone.1), window={size=1x1x128 pad=0_0x0_0x127_0}, to_apply=%region_0.0 | reduce-window | flops 2080768 | bytes 131076 | tf_op jit(solution)/shard_map/reduce-window
  6.4 0.1 slice.12
  6.4 0.1 copy.37
  6.6 0.1 copy.38
  6.7 0.1 add_add_fusion
  6.8 0.1 copy.34
  6.9 0.1 mul.36
  7.0 24.1 %scatter_custom_fusion = bf16[1536,2048]{1,0:T(8,128)(2,1)} fusion(s32[1024]{0:T(1024)S(1)} %bitcast.44, bf16[128,2048]{1,0:T(8,128)(2,1)} %param.6, s32[1024]{0:T(1024)S(1)} %broadcast_clamp_fusion.1, bf16[]{:T(256)} %constant.28.clone.1), kind=kCustom, calls=%fused_computation.7 | custom fusion | bytes 6291968 | tf_op jit(solution)/shard_map/scatter | solution.py:27
  31.1 10.4 %all_to_all.20 = bf16[2,8,96,2048]{3,2,1,0:T(8,128)(2,1)S(1)} all-to-all(bf16[2,8,96,2048]{3,2,1,0:T(8,128)(2,1)} %bitcast.37), channel_id=1, replica_groups=mesh['rep'=2,'grp'=2,'ep'=8] {'grp'}, dimensions={0} | all-to-all | bytes 12582912 | tf_op jit(solution)/shard_map/all_to_all | solution.py:30
  41.5 1.1 copy.39
  42.7 145.4 %all_to_all.21 = bf16[2,8,96,2048]{3,2,0,1:T(8,128)(2,1)S(1)} all-to-all(bf16[2,8,96,2048]{3,2,0,1:T(8,128)(2,1)S(1)} %copy.39), channel_id=1, replica_groups=mesh['rep'=2,'grp'=2,'ep'=8] {'ep'}, dimensions={1} | all-to-all | bytes 12582912 | tf_op jit(solution)/shard_map/all_to_all | solution.py:29
  188.0 0.0 copy-start.3
  188.0 1.1 copy.40
  189.2 0.8 copy-done.3
  189.9 0.0 copy-start.4
  189.9 5.3 %fusion.5 = f32[1536,768]{1,0:T(8,128)S(1)} fusion(bf16[1536,2048]{1,0:T(8,128)(2,1)S(1)} %bitcast.38, bf16[1,2048,768]{2,1,0:T(8,128)(2,1)S(1)} %copy-done.3), kind=kOutput, calls=%fused_computation.11 | convolution fusion | flops 4831838208 | bytes 14155776 | tf_op jit(solution)/shard_map/dot_general | solution.py:8
  195.2 0.0 copy-done.4
  195.2 5.6 %multiply_convert_fusion = bf16[1536,768]{1,0:T(8,128)(2,1)S(1)} fusion(f32[1536,768]{1,0:T(8,128)S(1)} %fusion.5, bf16[1536,2048]{1,0:T(8,128)(2,1)S(1)} %bitcast.39, bf16[1,2048,768]{2,1,0:T(8,128)(2,1)S(1)} %copy-done.4), kind=kOutput, calls=%fused_computation.6 | convolution fusion | flops 4838916096 | bytes 16515072 | tf_op jit(solution)/shard_map/dot_general | solution.py:9
  200.8 0.0 copy-done
  200.8 5.4 %convolution_convert_fusion = bf16[1536,2048]{1,0:T(8,128)(2,1)S(1)} fusion(bf16[1536,768]{1,0:T(8,128)(2,1)S(1)} %multiply_convert_fusion, bf16[1,768,2048]{2,1,0:T(8,128)(2,1)S(1)} %copy-done), kind=kOutput, calls=%fused_computation.5 | convolution fusion | flops 4834983936 | bytes 11796480 | tf_op jit(solution)/shard_map/dot_general | solution.py:11
  206.3 8.8 %all_to_all.22 = bf16[2,8,96,2048]{3,2,1,0:T(8,128)(2,1)S(1)} all-to-all(bf16[2,8,96,2048]{3,2,1,0:T(8,128)(2,1)S(1)} %bitcast.40), channel_id=1, replica_groups=mesh['rep'=2,'grp'=2,'ep'=8] {'grp'}, dimensions={0} | all-to-all | bytes 12582912 | tf_op jit(solution)/shard_map/all_to_all | solution.py:39
  215.1 3.2 copy.41
  218.3 0.0 copy-start.2
  218.3 5.1 %all-to-all-start.3 = ((bf16[2,8,96,2048]{3,2,0,1:T(8,128)(2,1)}), bf16[2,8,96,2048]{3,2,0,1:T(8,128)(2,1)}, u32[]{:S(2)}, u32[]{:S(2)}) async-start(bf16[2,8,96,2048]{3,2,0,1:T(8,128)(2,1)} %copy.41), calls=%async_computation.3 | async-start | bytes 12582912 | tf_op jit(solution)/shard_map/all_to_all | solution.py:38
  223.4 0.0 copy-done.2
  223.4 0.1 copy.43
  223.5 138.4 %all-to-all-done.3 = bf16[2,8,96,2048]{3,2,0,1:T(8,128)(2,1)} async-done(((bf16[2,8,96,2048]{3,2,0,1:T(8,128)(2,1)}), bf16[2,8,96,2048]{3,2,0,1:T(8,128)(2,1)}, u32[]{:S(2)}, u32[]{:S(2)}) %all-to-all-start.3) | async-done | bytes 6291488 | tf_op jit(solution)/shard_map/all_to_all | solution.py:38
  361.9 6.6 %copy.42 = bf16[2,8,96,2048]{3,2,1,0:T(8,128)(2,1)} copy(bf16[2,8,96,2048]{3,2,0,1:T(8,128)(2,1)} %all-to-all-done.3) | data formatting | bytes 12582912 | tf_op jit(solution)/shard_map/all_to_all | solution.py:38
  368.4 0.0 copy-start.1
  368.5 12.6 %gather_fusion = bf16[1024,2048]{1,0:T(8,128)(2,1)} fusion(bf16[1536,2048]{1,0:T(8,128)(2,1)} %bitcast.36, s32[1024]{0:T(1024)S(1)} %broadcast_clamp_fusion), kind=kCustom, calls=%fused_computation.1 | custom fusion | bytes 8392704 | tf_op jit(solution)/shard_map/gather | solution.py:45
  381.0 7.3 %fusion = bf16[128,2048]{1,0:T(8,128)(2,1)} fusion(bf16[1024,2048]{1,0:T(8,128)(2,1)} %gather_fusion, f32[128,8]{1,0:T(8,128)S(1)} %copy.43), kind=kLoop, calls=%fused_computation.4 | loop fusion | flops 6029312 | bytes 4722688 | tf_op jit(solution)/shard_map/reduce_sum | solution.py:47
  388.3 0.0 copy-done.1
  (8 shorter events, 0.1 us)
Async XLA Ops:
  0.0 200.8 %copy-start = (bf16[1,768,2048]{2,1,0:T(8,128)(2,1)S(1)}, bf16[1,768,2048]{2,1,0:T(8,128)(2,1)}, u32[]{:S(2)}) copy-start(bf16[1,768,2048]{2,1,0:T(8,128)(2,1)} %param.11) | copy-start | bytes 9437188
  188.0 1.9 copy-start.3
  189.9 5.3 %copy-start.4 = (bf16[1,2048,768]{2,1,0:T(8,128)(2,1)S(1)}, bf16[1,2048,768]{2,1,0:T(8,128)(2,1)}, u32[]{:S(2)}) copy-start(bf16[1,2048,768]{2,1,0:T(8,128)(2,1)} %param.10) | copy-start | bytes 9437188
  218.3 5.1 %copy-start.2 = (f32[128,8]{0,1:T(8,128)S(1)}, f32[128,8]{0,1:T(8,128)}, u32[]{:S(2)}) copy-start(f32[128,8]{0,1:T(8,128)} %param.8) | copy-start | bytes 12292
  218.3 143.6 %all-to-all-start.3 = ((bf16[2,8,96,2048]{3,2,0,1:T(8,128)(2,1)}), bf16[2,8,96,2048]{3,2,0,1:T(8,128)(2,1)}, u32[]{:S(2)}, u32[]{:S(2)}) async-start(bf16[2,8,96,2048]{3,2,0,1:T(8,128)(2,1)} %copy.41), calls=%async_computation.3 | async-start | bytes 12582912 | tf_op jit(solution)/shard_map/all_to_all | solution.py:38
  368.4 19.9 %copy-start.1 = (bf16[1,768,2048]{2,1,0:T(8,128)(2,1)S(1)}, bf16[1,768,2048]{2,1,0:T(8,128)(2,1)}, u32[]{:S(2)}) copy-start(bf16[1,768,2048]{2,1,0:T(8,128)(2,1)} %param.11) | copy-start | bytes 9437188
where the time goes:
time: 389 us; the launch traced here: 388 us
  blocking collectives  165 us (42%)
  waiting for transfers between devices  138 us (35%)
  local copies, waits for them, and re-layouts  51.2 us (13%)
  matrix products  16.3 us (4%)
  other arithmetic  12.7 us (3%)
  starting transfers between devices  5.09 us (1%)
    all_to_all x1, blocking collectives, local(): lax.all_to_all(lax.all_to_all(sectioned, 'grp', split_axis=0, concat_axis...  145 us
    all_to_all x1, waiting for transfers between devices, local(): lax.all_to_all(lax.all_to_all(results, 'grp', split_axis=0, concat_axis=0...  138 us
    scatter x1, local copies, waits for them, and re-layouts, local(): jnp.zeros((experts * capacity, width), jnp.bfloat16).at[position]  24.1 us
    gather x1, local copies, waits for them, and re-layouts, local(): back.reshape(experts * capacity, width)[position].astype(jnp.float32)  12.6 us
    all_to_all x1, blocking collectives, local(): lax.all_to_all(sectioned, 'grp', split_axis=0, concat_axis=0, tiled=True)  10.4 us
    all_to_all x1, blocking collectives, local(): lax.all_to_all(results, 'grp', split_axis=0, concat_axis=0, tiled=True)  8.79 us
  transfers between devices with their start and end apart: 1, of which 1 were waited for; matrix products, arithmetic and copies ran while one was open for 0% of the time, Pallas kernels for 0%

commit v1 on v0

--- a/solution.py
+++ b/solution.py
@@ -11,7 +11,7 @@
     return jnp.dot(hidden, w_down[0], preferred_element_type=jnp.float32).astype(jnp.bfloat16)
 
 
-def local(tokens, routes, gates, w_gate, w_up, w_down):
+def routed(tokens, routes, gates, w_gate, w_up, w_down):
     tok_rows, width = tokens.shape
     top = routes.shape[1]
     groups = lax.axis_size("grp")
@@ -48,7 +48,31 @@
     return mixed.astype(jnp.bfloat16)
 
 
+def gathered(tokens, routes, gates, w_gate, w_up, w_down):
+    axes = ("grp", "ep")
+    experts = lax.axis_size("grp") * lax.axis_size("ep")
+    me = lax.axis_index("grp") * lax.axis_size("ep") + lax.axis_index("ep")
+    ids = jnp.arange(experts, dtype=jnp.int32)
+    share = jnp.sum(jnp.where(routes[:, :, None] == ids, gates[:, :, None], 0.0), axis=1)
+    shares = lax.all_gather(share, axes, axis=0, tiled=True)
+    mine = jnp.sum(jnp.where(ids == me, shares, 0.0), axis=1, keepdims=True)
+    rows = lax.all_gather(tokens, axes, axis=0, tiled=True)
+    gate_act = jnp.dot(rows, w_gate[0], preferred_element_type=jnp.float32)
+    up_act = jnp.dot(rows, w_up[0], preferred_element_type=jnp.float32)
+    hidden = (jax.nn.silu(gate_act) * up_act).astype(jnp.bfloat16)
+    out = jnp.dot(hidden, w_down[0], preferred_element_type=jnp.float32)
+    part = (out * mine).astype(jnp.bfloat16)
+    return lax.psum_scatter(part, axes, scatter_dimension=0, tiled=True)
+
+
 def solution(mesh):
+    experts = mesh.shape["grp"] * mesh.shape["ep"]
+
+    def local(tokens, routes, gates, w_gate, w_up, w_down):
+        dense = routes.shape[1] * 3 >= experts
+        body = gathered if dense else routed
+        return body(tokens, routes, gates, w_gate, w_up, w_down)
+
     return jax.shard_map(
         local,
         mesh=mesh,

time: 389 us -> 230 us (0.59)
  blocking collectives: 165 us -> 35.8 us
  local copies, waits for them, and re-layouts: 51.2 us -> 0.01 us
  matrix products: 16.3 us -> 32.3 us
  between operations: 0.13 us -> 13.4 us
  other arithmetic: 12.7 us -> 0.99 us
  waiting for transfers between devices: 138 us -> 148 us
  starting transfers between devices: 5.09 us -> 0.04 us
    all_to_all x3 -> x0, blocking collectives: 165 us -> none  [the longest x1 145 us: local(): lax.all_to_all(lax.all_to_all(sectioned, 'grp', split_axis=0, concat_axis...]
    all_to_all x1 -> x0, waiting for transfers between devices: 138 us -> none  [local(): lax.all_to_all(lax.all_to_all(results, 'grp', split_axis=0, concat_axis=0...]
    reduce_scatter x0 -> x1, waiting for transfers between devices: none -> 103 us  [gathered(): return lax.psum_scatter(part, axes, scatter_dimension=0, tiled=True)]
    all_gather x0 -> x1, waiting for transfers between devices: none -> 43.9 us  [gathered(): rows = lax.all_gather(tokens, axes, axis=0, tiled=True)]
    all_gather x0 -> x1, blocking collectives: none -> 35.8 us  [gathered(): shares = lax.all_gather(share, axes, axis=0, tiled=True)]
    scatter x1 -> x0, local copies, waits for them, and re-layouts: 24.1 us -> none  [local(): jnp.zeros((experts * capacity, width), jnp.bfloat16).at[position]]
    dot_general x3 -> x2, matrix products: 16.3 us -> 32.3 us  [the longest x1 20.6 us: gathered(): out = jnp.dot(hidden, w_down[0], preferred_element_type=jnp.float32)]
    gather x1 -> x0, local copies, waits for them, and re-layouts: 12.6 us -> none  [local(): back.reshape(experts * capacity, width)[position].astype(jnp.float32)]
  transfers between devices with their start and end apart: 1 -> 2, of which waited for: 1 -> 2; matrix products, arithmetic and copies ran while one was open for 0% -> 0% of each run, Pallas kernels for 0% -> 0%
where the time goes in v1:
time: 230 us
  waiting for transfers between devices  148 us (64%)
  blocking collectives  35.8 us (16%)
  matrix products  32.3 us (14%)
  between operations  13.4 us (6%)
    reduce_scatter x1, waiting for transfers between devices, gathered(): return lax.psum_scatter(part, axes, scatter_dimension=0, tiled=True)  103 us
    all_gather x1, waiting for transfers between devices, gathered(): rows = lax.all_gather(tokens, axes, axis=0, tiled=True)  43.9 us
    all_gather x1, blocking collectives, gathered(): shares = lax.all_gather(share, axes, axis=0, tiled=True)  35.8 us
    dot_general x1, matrix products, gathered(): out = jnp.dot(hidden, w_down[0], preferred_element_type=jnp.float32)  20.6 us
    dot_general x1, matrix products, gathered(): gate_act = jnp.dot(rows, w_gate[0], preferred_element_type=jnp.float32)  11.7 us
  transfers between devices with their start and end apart: 2, of which 2 were waited for; matrix products, arithmetic and copies ran while one was open for 0% of the time, Pallas kernels for 0%

profile of v1, /device:TPU:0, one launch (start us, length us, event | category | flops | bytes accessed | tf_op | source)
XLA Modules:
  0.0 230.2 jit_solution(1227846433767845094)
XLA Ops:
  6.5 0.0 copy-start
  6.5 0.0 all-gather.2.cloned.1.call-start
  6.5 0.7 all-gather.2.cloned.1.call-update
  7.3 0.0 reduce-scatter.2.cloned.1.call-start
  7.3 0.9 select_reduce_fusion.1
  8.2 35.8 %all_gather.7 = f32[2048,16]{0,1:T(8,128)S(1)} all-gather(f32[128,16]{0,1:T(8,128)S(1)} %select_reduce_fusion.1), channel_id=1, replica_groups=mesh['rep'=2,'grp'=2,'ep'=8] {'grp','ep'}, dimensions={0}, use_global_device_ids=true | all-gather | bytes 139264 | tf_op jit(solution)/shard_map/all_gather | solution.py:57
  44.0 0.1 select_reduce_fusion
  44.1 43.9 %all-gather.2.cloned.1.call-done = bf16[2048,2048]{1,0:T(8,128)(2,1)} async-done(((bf16[128,2048]{1,0:T(8,128)(2,1)}), bf16[2048,2048]{1,0:T(8,128)(2,1)}) %all-gather.2.cloned.1.call-update) | async-done | bytes 8388624 | tf_op jit(solution)/shard_map/all_gather | solution.py:59
  88.0 11.7 %fusion.3 = f32[2048,768]{1,0:T(8,128)} fusion(bf16[2048,2048]{1,0:T(8,128)(2,1)} %all-gather.2.cloned.1.call-done, bf16[1,2048,768]{2,1,0:T(8,128)(2,1)} %param.9), kind=kOutput, calls=%fused_computation.4 | convolution fusion | flops 6442450944 | bytes 17825792 | tf_op jit(solution)/shard_map/dot_general | solution.py:60
  99.7 0.0 copy-done
  99.7 20.6 %multiply_convert_fusion = bf16[2048,2048]{1,0:T(8,128)(2,1)} fusion(f32[2048]{0:T(1024)S(1)} %select_reduce_fusion, f32[2048,768]{1,0:T(8,128)} %fusion.3, bf16[2048,2048]{1,0:T(8,128)(2,1)} %all-gather.2.cloned.1.call-done, bf16[1,768,2048]{2,1,0:T(8,128)(2,1)S(1)} %copy-done, bf16[1,2048,768]{2,1,0:T(8,128)(2,1)} %param.10), kind=kOutput, calls=%fused_computation | convolution fusion | flops 12902727680 | bytes 29368320 | tf_op jit(solution)/shard_map/dot_general | solution.py:63
  120.3 0.0 reduce-scatter.2.cloned.1.call-update
  120.4 103.0 %reduce-scatter.2.cloned.1.call-done = bf16[128,2048]{1,0:T(8,128)(2,1)} async-done(((bf16[2048,2048]{1,0:T(8,128)(2,1)}), bf16[128,2048]{1,0:T(8,128)(2,1)}) %reduce-scatter.2.cloned.1.call-update) | async-done | bytes 524304 | tf_op jit(solution)/shard_map/reduce_scatter | solution.py:65
  (1 shorter events, 0.0 us)
Async XLA Ops:
  6.5 93.2 %copy-start = (bf16[1,768,2048]{2,1,0:T(8,128)(2,1)S(1)}, bf16[1,768,2048]{2,1,0:T(8,128)(2,1)}, u32[]{:S(2)}) copy-start(bf16[1,768,2048]{2,1,0:T(8,128)(2,1)} %param.11) | copy-start | bytes 9437188
  6.5 81.5 %all-gather.2.cloned.1.call-start = ((), (), s32[]{:S(2)}) async-start(), calls=%async_computation.1 | async-start | bytes 8912896 | tf_op jit(solution)/shard_map/all_gather | solution.py:59
  7.3 216.1 %reduce-scatter.2.cloned.1.call-start = ((), (), s32[]{:S(2)}) async-start(), calls=%async_computation.2 | async-start | bytes 8912896 | tf_op jit(solution)/shard_map/reduce_scatter | solution.py:65
Sparse Core Ops, SparseCore 0:
  9.6 78.4 all-gather.1
  120.5 102.8 reduce-scatter.1

commit v2 on v0

--- a/solution.py
+++ b/solution.py
@@ -1,7 +1,11 @@
 import jax
 import jax.numpy as jnp
 from jax import lax
+from jax.experimental import pallas as pl
+from jax.experimental.pallas import tpu as pltpu
 from jax.sharding import PartitionSpec as P
+
+B_SHARE = 4
 
 
 def expert_rows(rows, w_gate, w_up, w_down):
@@ -11,7 +15,7 @@
     return jnp.dot(hidden, w_down[0], preferred_element_type=jnp.float32).astype(jnp.bfloat16)
 
 
-def local(tokens, routes, gates, w_gate, w_up, w_down):
+def routed(tokens, routes, gates, w_gate, w_up, w_down):
     tok_rows, width = tokens.shape
     top = routes.shape[1]
     groups = lax.axis_size("grp")
@@ -48,7 +52,301 @@
     return mixed.astype(jnp.bfloat16)
 
 
+def mixing_kernel(tokens_ref, shares_ref, wg_hbm, wu_hbm, wd_hbm, out_ref,
+                  xbuf, sbuf, wg, wu, wd, hid, scale, own, ysend, yrecv, zsend, zrecv, bsend, brecv,
+                  s_load, s_wsend, s_wrecv, s_ssend, s_srecv,
+                  s_zs1, s_zs2, s_zr1, s_zr2, s_yas, s_yar, s_ybs, s_ybr,
+                  s_pys, s_pyr, s_pzs, s_pzr, s_pbs, s_pbr):
+    rows = tokens_ref.shape[0]
+    row_b = brecv.shape[1]
+    row_a = rows - row_b
+    kept = row_a + 2 * row_b
+    hidden = wg.shape[2]
+    chunks, _, wide = bsend.shape
+    planes = xbuf.shape[0]
+    last = planes - 1
+    members = 2 * planes
+    me = lax.axis_index("ep")
+    core = lax.axis_index("grp")
+    z, y = me // 2, me % 2
+    twin = {"grp": 1 - core}
+    across = {"ep": z * 2 + (1 - y)}
+    end = (z == 0) | (z == last)
+    inner = jnp.logical_not(end)
+    low = z < planes // 2
+
+    def remote(src, dst, send, recv, to):
+        return pltpu.make_async_remote_copy(src_ref=src, dst_ref=dst, send_sem=send, recv_sem=recv, device_id=to,
+                                            device_id_type=pl.DeviceIdType.MESH)
+
+    barrier = pltpu.get_barrier_semaphore()
+    pl.semaphore_signal(barrier, inc=1, device_id=twin, device_id_type=pl.DeviceIdType.MESH)
+    for k in range(1, members):
+        pl.semaphore_signal(barrier, inc=1, device_id={"ep": lax.rem(me + k, members)}, device_id_type=pl.DeviceIdType.MESH)
+
+    loads = [pltpu.make_async_copy(tokens_ref, xbuf.at[z, pl.ds(0, rows)], s_load.at[0]),
+             pltpu.make_async_copy(wg_hbm.at[0], wg.at[0], s_load.at[1]),
+             pltpu.make_async_copy(wu_hbm.at[0], wu.at[0], s_load.at[2]),
+             pltpu.make_async_copy(wd_hbm.at[0], wd.at[pl.ds(0, hidden)], s_load.at[3])]
+    for copy in loads:
+        copy.start()
+    pl.semaphore_wait(barrier, members)
+
+    rng_a, rng_b = pl.ds(0, row_a), pl.ds(row_a, row_b)
+    rng_ob, rng_oa = pl.ds(rows, row_b), pl.ds(rows + row_b, row_a)
+
+    def hop1(p, slot, step, src):
+        return remote(src, xbuf.at[p, pl.ds(0, rows)], s_zs1.at[slot], s_zr1.at[p], {"ep": (z + step) * 2 + y})
+
+    def hop2(p, slot, step):
+        return remote(xbuf.at[p, rng_ob], xbuf.at[p, rng_ob], s_zs2.at[slot], s_zr2.at[p], {"ep": (z + step) * 2 + y})
+
+    def cross_a(p, src):
+        return remote(src, xbuf.at[p, rng_oa], s_yas.at[p], s_yar.at[p], across)
+
+    own_b = remote(tokens_ref.at[rng_b], xbuf.at[z, rng_ob], s_ybs.at[0], s_ybr.at[0], across)
+    own_b.start()
+
+    def both(make, act):
+        pl.when(z < last)(lambda: act(make(z, 1)))
+        pl.when(z > 0)(lambda: act(make(planes, -1)))
+
+    first1 = lambda slot, step: hop1(z, slot, step, tokens_ref)
+    first2 = lambda slot, step: hop2(z, slot, step)
+    both(first1, lambda c: c.start())
+    own_a = cross_a(z, tokens_ref.at[rng_a])
+    own_a.start()
+
+    def share_copy(k):
+        to = lax.rem(me + k, members)
+        return remote(shares_ref.at[to], sbuf.at[me], s_ssend.at[k], s_srecv.at[k], {"ep": to})
+
+    for k in range(1, members):
+        share_copy(k).start()
+    sbuf[me] = shares_ref[me]
+    weights = [remote(wg_hbm.at[0], wg.at[1], s_wsend.at[0], s_wrecv.at[0], twin),
+               remote(wu_hbm.at[0], wu.at[1], s_wsend.at[1], s_wrecv.at[1], twin),
+               remote(wd_hbm.at[0], wd.at[pl.ds(hidden, hidden)], s_wsend.at[2], s_wrecv.at[2], twin)]
+    for copy in weights:
+        copy.start()
+
+    own_b.wait_recv()
+    both(first2, lambda c: c.start())
+
+    def order(s):
+        if planes == 2:
+            near = s
+        else:
+            near = jnp.where(end, s, jnp.where(s == 0, 1, jnp.where(s == 1, 0, s)))
+        return jnp.where(low, near, last - near)
+
+    def forward(p, act1, act2):
+        pl.when((p < z) & (z < last))(lambda: act1(hop1(p, p, 1, xbuf.at[p, pl.ds(0, rows)]), hop2(p, p, 1)))
+        pl.when((p > z) & (z > 0))(lambda: act1(hop1(p, p, -1, xbuf.at[p, pl.ds(0, rows)]), hop2(p, p, -1)))
+
+    def relay(s):
+        p = order(s)
+        hop1(p, p, 0, xbuf.at[p, pl.ds(0, rows)]).wait_recv()
+        forward(p, lambda a, b: a.start(), None)
+        cross_a(p, xbuf.at[p, rng_a]).start()
+        hop2(p, p, 0).wait_recv()
+        forward(p, lambda a, b: b.start(), None)
+
+    def column(src, e):
+        line = sbuf[src, pl.ds(e, 1), :]
+        diag = lax.broadcasted_iota(jnp.int32, (rows, rows), 0) == lax.broadcasted_iota(jnp.int32, (rows, rows), 1)
+        return jnp.sum(jnp.where(diag, jnp.broadcast_to(line, (rows, rows)), 0.0), axis=1, keepdims=True)
+
+    def arrived(p):
+        cross_a(p, xbuf.at[p, rng_a]).wait_recv()
+        for e in range(2):
+            scale[e, pl.ds(0, rows), :] = jnp.broadcast_to(column(p * 2 + y, e), (rows, 128))
+            other = jnp.broadcast_to(column(p * 2 + 1 - y, e), (rows, 128))
+            scale[e, rng_ob, :] = other[row_a:]
+            scale[e, rng_oa, :] = other[:row_a]
+
+    tile = 256
+
+    def make_hidden(p, e):
+        @pl.loop(0, hidden // tile)
+        def _(t):
+            cols = pl.ds(pl.multiple_of(t * tile, tile), tile)
+            x = xbuf[p]
+            g = jnp.dot(x, wg[e, :, cols], preferred_element_type=jnp.float32)
+            u = jnp.dot(x, wu[e, :, cols], preferred_element_type=jnp.float32)
+            h = g / (1.0 + jnp.exp(-g)) * u * scale[e, :, pl.ds(0, 1)]
+            hid[:, pl.ds(pl.multiple_of(e * hidden + t * tile, tile), tile)] = h.astype(jnp.bfloat16)
+
+    def part_y(p, n):
+        return remote(ysend.at[p, n], yrecv.at[p, n], s_pys.at[p, n], s_pyr.at[p, n], across)
+
+    def make_down(p):
+        @pl.loop(0, chunks)
+        def _(n):
+            acc = jnp.dot(hid[...], wd[:, pl.ds(pl.multiple_of(n * wide, wide), wide)], preferred_element_type=jnp.float32)
+            ysend[p, n] = acc[kept:].astype(jnp.bfloat16)
+            part_y(p, n).start()
+            own[p, n] = acc[:kept]
+
+    def part_z(p, n, step):
+        slot = jnp.where((step < 0) & (z + step == p), planes, p)
+        return remote(zsend.at[p, n], zrecv.at[slot, n], s_pzs.at[p, n], s_pzr.at[slot, n], {"ep": (z + step) * 2 + y})
+
+    def from_z(slot, n):
+        remote(zsend.at[0, n], zrecv.at[slot, n], s_pzs.at[0, n], s_pzr.at[slot, n], across).wait_recv()
+        own_p = jnp.where(slot == planes, z, slot)
+        own[own_p, n] = own[own_p, n] + zrecv[slot, n].astype(jnp.float32)
+
+    def toward(p, act):
+        pl.when(p < z)(lambda: act(-1))
+        pl.when(p > z)(lambda: act(1))
+
+    def add_y(p, n):
+        part_y(p, n).wait_recv()
+        own[p, n, pl.ds(0, row_a), :] = own[p, n, pl.ds(0, row_a), :] + yrecv[p, n].astype(jnp.float32)
+
+    def reduce_on(p, n):
+        add_y(p, n)
+
+        @pl.when(inner)
+        def _():
+            from_z(p, n)
+
+        zsend[p, n] = own[p, n].astype(jnp.bfloat16)
+        toward(p, lambda step: part_z(p, n, step).start())
+
+    for copy in loads:
+        copy.wait()
+    for k in range(1, members):
+        share_copy(k).wait_recv()
+    arrived(z)
+    make_hidden(z, 0)
+    relay(1)
+    pl.when(inner)(lambda: relay(2))
+    for copy in weights:
+        copy.wait_recv()
+    make_hidden(z, 1)
+    make_down(z)
+
+    @pl.loop(1, planes)
+    def _(s):
+        p = order(s)
+        pl.when(((s == 2) & end) | (s == 3))(lambda: relay(s))
+        arrived(p)
+        pl.loop(0, 2)(lambda e: make_hidden(p, e))
+        make_down(p)
+
+        @pl.when(end)
+        def _():
+            pl.loop(0, chunks)(lambda n: reduce_on(p, n))
+
+    @pl.when(inner)
+    def _():
+        near = jnp.where(low, 0, last)
+        pl.loop(0, chunks)(lambda n: reduce_on(last - z, n))
+
+        @pl.loop(0, chunks)
+        def _(n):
+            reduce_on(last - near, n)
+            reduce_on(near, n)
+
+    def part_b(n):
+        return remote(bsend.at[n], brecv.at[n], s_pbs.at[n], s_pbr.at[n], across)
+
+    @pl.loop(0, chunks)
+    def _(n):
+        add_y(z, n)
+        pl.when(z > 0)(lambda: from_z(z, n))
+        pl.when(z < last)(lambda: from_z(planes, n))
+        bsend[n] = own[z, n, rng_ob, :].astype(jnp.bfloat16)
+        part_b(n).start()
+
+    for n in range(chunks):
+        part_b(n).wait_recv()
+        cols = pl.ds(n * wide, wide)
+        out_ref[rng_a, cols] = own[z, n, rng_a, :].astype(jnp.bfloat16)
+        out_ref[rng_b, cols] = (own[z, n, rng_b, :] + brecv[n].astype(jnp.float32)).astype(jnp.bfloat16)
+
+    own_b.wait_send()
+    both(first1, lambda c: c.wait_send())
+    both(first2, lambda c: c.wait_send())
+    for k in range(1, members):
+        share_copy(k).wait_send()
+    for copy in weights:
+        copy.wait_send()
+
+    def both_sent(a, b):
+        a.wait_send()
+        b.wait_send()
+
+    @pl.loop(0, planes)
+    def _(p):
+        cross_a(p, xbuf.at[p, rng_a]).wait_send()
+        forward(p, both_sent, None)
+
+        @pl.loop(0, chunks)
+        def _(n):
+            part_y(p, n).wait_send()
+            toward(p, lambda step: part_z(p, n, step).wait_send())
+
+    for n in range(chunks):
+        part_b(n).wait_send()
+
+
+def fused(tokens, routes, gates, w_gate, w_up, w_down):
+    rows, width = tokens.shape
+    hidden = w_gate.shape[2]
+    members = lax.axis_size("ep")
+    planes = members // 2
+    row_b = rows * B_SHARE // 8
+    row_a = rows - row_b
+    kept = row_a + 2 * row_b
+    chunks = 4
+    wide = width // chunks
+    core = lax.axis_index("grp")
+    ids = lax.rem(core + jnp.arange(8, dtype=jnp.int32), 2)[None, :] * members + jnp.arange(members, dtype=jnp.int32)[:, None]
+    shares = jnp.sum(jnp.where(routes.T[:, None, None, :] == ids[None, :, :, None], gates.T[:, None, None, :], 0.0), axis=0)
+    bf, dma = jnp.bfloat16, pltpu.SemaphoreType.DMA
+    flops = 2 * members * rows * width * hidden * 6
+    return pl.pallas_call(
+        mixing_kernel,
+        out_shape=jax.ShapeDtypeStruct((rows, width), bf),
+        in_specs=[pl.BlockSpec(memory_space=pltpu.VMEM)] * 2 + [pl.BlockSpec(memory_space=pl.ANY)] * 3,
+        out_specs=pl.BlockSpec(memory_space=pltpu.VMEM),
+        scratch_shapes=[
+            pltpu.VMEM((planes, 2 * rows, width), bf),
+            pltpu.VMEM((members, 8, rows), jnp.float32),
+            pltpu.VMEM((2, width, hidden), bf),
+            pltpu.VMEM((2, width, hidden), bf),
+            pltpu.VMEM((2 * hidden, width), bf),
+            pltpu.VMEM((2 * rows, 2 * hidden), bf),
+            pltpu.VMEM((2, 2 * rows, 128), jnp.float32),
+            pltpu.VMEM((planes, chunks, kept, wide), jnp.float32),
+            pltpu.VMEM((planes, chunks, row_a, wide), bf),
+            pltpu.VMEM((planes, chunks, row_a, wide), bf),
+            pltpu.VMEM((planes, chunks, kept, wide), bf),
+            pltpu.VMEM((planes + 1, chunks, kept, wide), bf),
+            pltpu.VMEM((chunks, row_b, wide), bf),
+            pltpu.VMEM((chunks, row_b, wide), bf),
+            dma((4,)), dma((3,)), dma((3,)), dma((members,)), dma((members,)),
+            dma((planes + 1,)), dma((planes + 1,)), dma((planes,)), dma((planes,)),
+            dma((planes,)), dma((planes,)), dma((1,)), dma((1,)),
+            dma((planes, chunks)), dma((planes, chunks)), dma((planes, chunks)), dma((planes + 1, chunks)),
+            dma((chunks,)), dma((chunks,)),
+        ],
+        compiler_params=pltpu.CompilerParams(collective_id=0, has_side_effects=True, vmem_limit_bytes=60 * 1024 * 1024),
+        cost_estimate=pl.CostEstimate(flops=flops, bytes_accessed=20 * 1024 * 1024, transcendentals=0),
+    )(tokens, shares, w_gate, w_up, w_down)
+
+
 def solution(mesh):
+    groups, members = mesh.shape["grp"], mesh.shape["ep"]
+
+    def local(tokens, routes, gates, w_gate, w_up, w_down):
+        dense = groups == 2 and members == 8 and routes.shape[1] * 3 >= groups * members
+        body = fused if dense else routed
+        return body(tokens, routes, gates, w_gate, w_up, w_down)
+
     return jax.shard_map(
         local,
         mesh=mesh,

time: 389 us -> 118 us (0.30)
  blocking collectives: 165 us -> 0 us
  waiting for transfers between devices: 138 us -> 0 us
  Pallas kernels: 0 us -> 115 us
  local copies, waits for them, and re-layouts: 51.2 us -> 1.88 us
  matrix products: 16.3 us -> 0 us
  other arithmetic: 12.7 us -> 1.43 us
  starting transfers between devices: 5.09 us -> 0 us
    all_to_all x3 -> x0, blocking collectives: 165 us -> none  [the longest x1 145 us: local(): lax.all_to_all(lax.all_to_all(sectioned, 'grp', split_axis=0, concat_axis...]
    all_to_all x1 -> x0, waiting for transfers between devices: 138 us -> none  [local(): lax.all_to_all(lax.all_to_all(results, 'grp', split_axis=0, concat_axis=0...]
    pallas_call x0 -> x1, Pallas kernels: none -> 115 us  [fused(): pl.pallas_call(mixing_kernel, out_shape=jax.ShapeDtypeStruct((rows, width...]
    scatter x1 -> x0, local copies, waits for them, and re-layouts: 24.1 us -> none  [local(): jnp.zeros((experts * capacity, width), jnp.bfloat16).at[position]]
    dot_general x3 -> x0, matrix products: 16.3 us -> none  [the longest x1 5.63 us: expert_rows(): up_act = jnp.dot(rows, w_up[0], preferred_element_type=jnp.float32)]
    gather x1 -> x0, local copies, waits for them, and re-layouts: 12.6 us -> none  [local(): back.reshape(experts * capacity, width)[position].astype(jnp.float32)]
    all_to_all x4 -> x0, local copies, waits for them, and re-layouts: 12 us -> none  [the longest x1 6.57 us: local(): lax.all_to_all(lax.all_to_all(results, 'grp', split_axis=0, concat_axis=0...]
    reduce_sum x2 -> x1, other arithmetic: 7.35 us -> 1.42 us  [fused(): jnp.sum(jnp.where(routes.T[:, None, None, :] == ids[None, :, :, None], ga...]
  transfers between devices with their start and end apart: 1 -> 0, of which waited for: 1 -> 0; matrix products, arithmetic and copies ran while one was open for 0% -> 0% of each run, Pallas kernels for 0% -> 0%
where the time goes in v2:
time: 118 us
  Pallas kernels  115 us (97%)
  local copies, waits for them, and re-layouts  1.88 us (2%)
  other arithmetic  1.43 us (1%)
    pallas_call x1, Pallas kernels, fused(): pl.pallas_call(mixing_kernel, out_shape=jax.ShapeDtypeStruct((rows, width...  115 us

profile of v2, /device:TPU:0, one launch (start us, length us, event | category | flops | bytes accessed | tf_op | source)
XLA Modules:
  0.0 118.2 jit_solution(3631703780146467596)
XLA Ops:
  0.0 1.4 %select_reduce_fusion.shares_ref = f32[8,8,128]{2,1,0:T(8,128)} fusion(f32[8,128]{1,0:T(8,128)} %bitcast.2, s32[8,8]{1,0:T(8,128)S(1)} %iota_add_fusion, s32[8,128]{1,0:T(8,128)} %bitcast.3), kind=kLoop, calls=%fused_computation | loop fusion | flops 188416 | bytes 41216 | tf_op jit(solution)/shard_map/reduce_sum | solution.py:308
  1.4 114.8 %shard_map.64 = bf16[128,2048]{1,0:T(8,128)(2,1)} custom-call(bf16[128,2048]{1,0:T(8,128)(2,1)} %tokens_ref.1, f32[8,8,128]{2,1,0:T(8,128)} %select_reduce_fusion.shares_ref, bf16[1,2048,768]{2,1,0:T(8,128)(2,1)} %wg_hbm.1, bf16[1,2048,768]{2,1,0:T(8,128)(2,1)} %wu_hbm.1, bf16[1,768,2048]{2,1,0:T(8,128)(2,1)} %wd_hbm.1), custom_call_target="tpu_custom_call" | custom-call | flops 19327352832 | bytes 20971520 | tf_op jit(solution)/shard_map/pallas_call | solution.py:311
  116.3 1.9 %copy.8 = bf16[128,2048]{1,0:T(8,128)(2,1)} copy(bf16[128,2048]{1,0:T(8,128)(2,1)} %shard_map.64) | data formatting | bytes 1048576
  (2 shorter events, 0.0 us)

commit v3 on v2

--- a/solution.py
+++ b/solution.py
@@ -53,14 +53,13 @@
 
 
 def mixing_kernel(tokens_ref, shares_ref, wg_hbm, wu_hbm, wd_hbm, out_ref,
-                  xbuf, sbuf, wg, wu, wd, hid, scale, own, ysend, yrecv, zsend, zrecv, bsend, brecv,
+                  xbuf, sbuf, wg, wu, wd, hid, scale, own, ysend, yrecv, zsend_a, zsend_b, zrecv_a, zrecv_b, bsend, brecv,
                   s_load, s_wsend, s_wrecv, s_ssend, s_srecv,
                   s_zs1, s_zs2, s_zr1, s_zr2, s_yas, s_yar, s_ybs, s_ybr,
-                  s_pys, s_pyr, s_pzs, s_pzr, s_pbs, s_pbr):
+                  s_pys, s_pyr, s_pzs_a, s_pzr_a, s_pzs_b, s_pzr_b, s_pbs, s_pbr):
     rows = tokens_ref.shape[0]
     row_b = brecv.shape[1]
     row_a = rows - row_b
-    kept = row_a + 2 * row_b
     hidden = wg.shape[2]
     chunks, _, wide = bsend.shape
     planes = xbuf.shape[0]
@@ -84,7 +83,14 @@
     for k in range(1, members):
         pl.semaphore_signal(barrier, inc=1, device_id={"ep": lax.rem(me + k, members)}, device_id_type=pl.DeviceIdType.MESH)
 
-    loads = [pltpu.make_async_copy(tokens_ref, xbuf.at[z, pl.ds(0, rows)], s_load.at[0]),
+    rng_a, rng_b = pl.ds(0, row_a), pl.ds(row_a, row_b)
+    rng_oa, rng_mb = pl.ds(row_a, row_a), pl.ds(2 * row_a, row_b)
+    rng_ob, rng_bb = pl.ds(2 * row_a + row_b, row_b), pl.ds(2 * row_a, 2 * row_b)
+    rng_aa = pl.ds(0, 2 * row_a)
+    own_bb = pl.ds(row_a, 2 * row_b)
+
+    loads = [pltpu.make_async_copy(tokens_ref.at[rng_b], xbuf.at[z, rng_mb], s_load.at[0]),
+             pltpu.make_async_copy(tokens_ref.at[rng_a], xbuf.at[z, rng_a], s_load.at[4]),
              pltpu.make_async_copy(wg_hbm.at[0], wg.at[0], s_load.at[1]),
              pltpu.make_async_copy(wu_hbm.at[0], wu.at[0], s_load.at[2]),
              pltpu.make_async_copy(wd_hbm.at[0], wd.at[pl.ds(0, hidden)], s_load.at[3])]
@@ -92,14 +98,11 @@
         copy.start()
     pl.semaphore_wait(barrier, members)
 
-    rng_a, rng_b = pl.ds(0, row_a), pl.ds(row_a, row_b)
-    rng_ob, rng_oa = pl.ds(rows, row_b), pl.ds(rows + row_b, row_a)
-
     def hop1(p, slot, step, src):
-        return remote(src, xbuf.at[p, pl.ds(0, rows)], s_zs1.at[slot], s_zr1.at[p], {"ep": (z + step) * 2 + y})
+        return remote(src, xbuf.at[p, rng_a], s_zs1.at[slot], s_zr1.at[p], {"ep": (z + step) * 2 + y})
 
     def hop2(p, slot, step):
-        return remote(xbuf.at[p, rng_ob], xbuf.at[p, rng_ob], s_zs2.at[slot], s_zr2.at[p], {"ep": (z + step) * 2 + y})
+        return remote(xbuf.at[p, rng_bb], xbuf.at[p, rng_bb], s_zs2.at[slot], s_zr2.at[p], {"ep": (z + step) * 2 + y})
 
     def cross_a(p, src):
         return remote(src, xbuf.at[p, rng_oa], s_yas.at[p], s_yar.at[p], across)
@@ -111,7 +114,7 @@
         pl.when(z < last)(lambda: act(make(z, 1)))
         pl.when(z > 0)(lambda: act(make(planes, -1)))
 
-    first1 = lambda slot, step: hop1(z, slot, step, tokens_ref)
+    first1 = lambda slot, step: hop1(z, slot, step, tokens_ref.at[rng_a])
     first2 = lambda slot, step: hop2(z, slot, step)
     both(first1, lambda c: c.start())
     own_a = cross_a(z, tokens_ref.at[rng_a])
@@ -130,6 +133,7 @@
     for copy in weights:
         copy.start()
 
+    loads[0].wait()
     own_b.wait_recv()
     both(first2, lambda c: c.start())
 
@@ -141,16 +145,19 @@
         return jnp.where(low, near, last - near)
 
     def forward(p, act1, act2):
-        pl.when((p < z) & (z < last))(lambda: act1(hop1(p, p, 1, xbuf.at[p, pl.ds(0, rows)]), hop2(p, p, 1)))
-        pl.when((p > z) & (z > 0))(lambda: act1(hop1(p, p, -1, xbuf.at[p, pl.ds(0, rows)]), hop2(p, p, -1)))
+        pl.when((p < z) & (z < last))(lambda: act1(hop1(p, p, 1, xbuf.at[p, rng_a]), hop2(p, p, 1)))
+        pl.when((p > z) & (z > 0))(lambda: act1(hop1(p, p, -1, xbuf.at[p, rng_a]), hop2(p, p, -1)))
 
     def relay(s):
         p = order(s)
-        hop1(p, p, 0, xbuf.at[p, pl.ds(0, rows)]).wait_recv()
+        hop1(p, p, 0, xbuf.at[p, rng_a]).wait_recv()
         forward(p, lambda a, b: a.start(), None)
         cross_a(p, xbuf.at[p, rng_a]).start()
-        hop2(p, p, 0).wait_recv()
-        forward(p, lambda a, b: b.start(), None)
+
+        @pl.when(inner)
+        def _():
+            hop2(p, p, 0).wait_recv()
+            forward(p, lambda a, b: b.start(), None)
 
     def column(src, e):
         line = sbuf[src, pl.ds(e, 1), :]
@@ -160,42 +167,39 @@
     def arrived(p):
         cross_a(p, xbuf.at[p, rng_a]).wait_recv()
         for e in range(2):
-            scale[e, pl.ds(0, rows), :] = jnp.broadcast_to(column(p * 2 + y, e), (rows, 128))
+            mine = jnp.broadcast_to(column(p * 2 + y, e), (rows, 128))
             other = jnp.broadcast_to(column(p * 2 + 1 - y, e), (rows, 128))
+            scale[e, rng_a, :] = mine[:row_a]
+            scale[e, rng_oa, :] = other[:row_a]
+            scale[e, rng_mb, :] = mine[row_a:]
             scale[e, rng_ob, :] = other[row_a:]
-            scale[e, rng_oa, :] = other[:row_a]
 
     tile = 256
 
-    def make_hidden(p, e):
+    def make_hidden(p, e, part):
         @pl.loop(0, hidden // tile)
         def _(t):
             cols = pl.ds(pl.multiple_of(t * tile, tile), tile)
-            x = xbuf[p]
+            x = xbuf[p, part, :]
             g = jnp.dot(x, wg[e, :, cols], preferred_element_type=jnp.float32)
             u = jnp.dot(x, wu[e, :, cols], preferred_element_type=jnp.float32)
-            h = g / (1.0 + jnp.exp(-g)) * u * scale[e, :, pl.ds(0, 1)]
-            hid[:, pl.ds(pl.multiple_of(e * hidden + t * tile, tile), tile)] = h.astype(jnp.bfloat16)
+            h = g / (1.0 + jnp.exp(-g)) * u * scale[e, part, pl.ds(0, 1)]
+            hid[part, pl.ds(pl.multiple_of(e * hidden + t * tile, tile), tile)] = h.astype(jnp.bfloat16)
 
     def part_y(p, n):
         return remote(ysend.at[p, n], yrecv.at[p, n], s_pys.at[p, n], s_pyr.at[p, n], across)
 
-    def make_down(p):
-        @pl.loop(0, chunks)
-        def _(n):
-            acc = jnp.dot(hid[...], wd[:, pl.ds(pl.multiple_of(n * wide, wide), wide)], preferred_element_type=jnp.float32)
-            ysend[p, n] = acc[kept:].astype(jnp.bfloat16)
-            part_y(p, n).start()
-            own[p, n] = acc[:kept]
-
-    def part_z(p, n, step):
+    def part_z(p, n, step, b):
         slot = jnp.where((step < 0) & (z + step == p), planes, p)
-        return remote(zsend.at[p, n], zrecv.at[slot, n], s_pzs.at[p, n], s_pzr.at[slot, n], {"ep": (z + step) * 2 + y})
-
-    def from_z(slot, n):
-        remote(zsend.at[0, n], zrecv.at[slot, n], s_pzs.at[0, n], s_pzr.at[slot, n], across).wait_recv()
+        src, dst, send, recv = (zsend_b, zrecv_b, s_pzs_b, s_pzr_b) if b else (zsend_a, zrecv_a, s_pzs_a, s_pzr_a)
+        return remote(src.at[p, n], dst.at[slot, n], send.at[p, n], recv.at[slot, n], {"ep": (z + step) * 2 + y})
+
+    def from_z(slot, n, b):
+        src, dst, send, recv = (zsend_b, zrecv_b, s_pzs_b, s_pzr_b) if b else (zsend_a, zrecv_a, s_pzs_a, s_pzr_a)
+        remote(src.at[0, n], dst.at[slot, n], send.at[0, n], recv.at[slot, n], across).wait_recv()
         own_p = jnp.where(slot == planes, z, slot)
-        own[own_p, n] = own[own_p, n] + zrecv[slot, n].astype(jnp.float32)
+        part = own_bb if b else rng_a
+        own[own_p, n, part, :] = own[own_p, n, part, :] + dst[slot, n].astype(jnp.float32)
 
     def toward(p, act):
         pl.when(p < z)(lambda: act(-1))
@@ -205,66 +209,100 @@
         part_y(p, n).wait_recv()
         own[p, n, pl.ds(0, row_a), :] = own[p, n, pl.ds(0, row_a), :] + yrecv[p, n].astype(jnp.float32)
 
-    def reduce_on(p, n):
+    def make_down(p, b):
+        part = rng_bb if b else rng_aa
+
+        @pl.loop(0, chunks)
+        def _(n):
+            acc = jnp.dot(hid[part, :], wd[:, pl.ds(pl.multiple_of(n * wide, wide), wide)], preferred_element_type=jnp.float32)
+            if b:
+                own[p, n, own_bb, :] = acc
+
+                @pl.when(end)
+                def _():
+                    zsend_b[p, n] = acc.astype(jnp.bfloat16)
+                    toward(p, lambda step: part_z(p, n, step, True).start())
+            else:
+                ysend[p, n] = acc[row_a:].astype(jnp.bfloat16)
+                part_y(p, n).start()
+                own[p, n, rng_a, :] = acc[:row_a]
+
+    def reduce_a(p, n):
         add_y(p, n)
-
-        @pl.when(inner)
-        def _():
-            from_z(p, n)
-
-        zsend[p, n] = own[p, n].astype(jnp.bfloat16)
-        toward(p, lambda step: part_z(p, n, step).start())
-
-    for copy in loads:
+        pl.when(inner)(lambda: from_z(p, n, False))
+        zsend_a[p, n] = own[p, n, rng_a, :].astype(jnp.bfloat16)
+        toward(p, lambda step: part_z(p, n, step, False).start())
+
+    def reduce_b(p, n):
+        from_z(p, n, True)
+        zsend_b[p, n] = own[p, n, own_bb, :].astype(jnp.bfloat16)
+        toward(p, lambda step: part_z(p, n, step, True).start())
+
+    for copy in loads[1:]:
         copy.wait()
     for k in range(1, members):
         share_copy(k).wait_recv()
     arrived(z)
-    make_hidden(z, 0)
+    make_hidden(z, 0, pl.ds(0, 2 * rows))
     relay(1)
     pl.when(inner)(lambda: relay(2))
     for copy in weights:
         copy.wait_recv()
-    make_hidden(z, 1)
-    make_down(z)
+    make_hidden(z, 1, pl.ds(0, 2 * rows))
+    make_down(z, False)
+    make_down(z, True)
 
     @pl.loop(1, planes)
     def _(s):
         p = order(s)
-        pl.when(((s == 2) & end) | (s == 3))(lambda: relay(s))
+        pl.when((s == 2) | ((s == 3) & end))(lambda: relay(jnp.where(inner, s + 1, s)))
         arrived(p)
-        pl.loop(0, 2)(lambda e: make_hidden(p, e))
-        make_down(p)
+        pl.loop(0, 2)(lambda e: make_hidden(p, e, rng_aa))
+        make_down(p, False)
+        pl.when(end)(lambda: hop2(p, p, 0).wait_recv())
+        pl.loop(0, 2)(lambda e: make_hidden(p, e, rng_bb))
+        make_down(p, True)
 
         @pl.when(end)
         def _():
-            pl.loop(0, chunks)(lambda n: reduce_on(p, n))
+            pl.loop(0, chunks)(lambda n: reduce_a(p, n))
 
     @pl.when(inner)
     def _():
         near = jnp.where(low, 0, last)
-        pl.loop(0, chunks)(lambda n: reduce_on(last - z, n))
+        pl.loop(0, chunks)(lambda n: reduce_b(last - z, n))
+        pl.loop(0, chunks)(lambda n: reduce_a(last - z, n))
 
         @pl.loop(0, chunks)
         def _(n):
-            reduce_on(last - near, n)
-            reduce_on(near, n)
+            reduce_b(last - near, n)
+            reduce_b(near, n)
+
+        @pl.loop(0, chunks)
+        def _(n):
+            reduce_a(last - near, n)
+            reduce_a(near, n)
 
     def part_b(n):
         return remote(bsend.at[n], brecv.at[n], s_pbs.at[n], s_pbr.at[n], across)
 
     @pl.loop(0, chunks)
     def _(n):
+        pl.when(z > 0)(lambda: from_z(z, n, True))
+        pl.when(z < last)(lambda: from_z(planes, n, True))
+        bsend[n] = own[z, n, pl.ds(row_a + row_b, row_b), :].astype(jnp.bfloat16)
+        part_b(n).start()
+
+    for n in range(chunks):
+        cols = pl.ds(n * wide, wide)
         add_y(z, n)
-        pl.when(z > 0)(lambda: from_z(z, n))
-        pl.when(z < last)(lambda: from_z(planes, n))
-        bsend[n] = own[z, n, rng_ob, :].astype(jnp.bfloat16)
-        part_b(n).start()
+        pl.when(z > 0)(lambda: from_z(z, n, False))
+        pl.when(z < last)(lambda: from_z(planes, n, False))
+        out_ref[rng_a, cols] = own[z, n, rng_a, :].astype(jnp.bfloat16)
 
     for n in range(chunks):
         part_b(n).wait_recv()
         cols = pl.ds(n * wide, wide)
-        out_ref[rng_a, cols] = own[z, n, rng_a, :].astype(jnp.bfloat16)
         out_ref[rng_b, cols] = (own[z, n, rng_b, :] + brecv[n].astype(jnp.float32)).astype(jnp.bfloat16)
 
     own_b.wait_send()
@@ -287,7 +325,7 @@
         @pl.loop(0, chunks)
         def _(n):
             part_y(p, n).wait_send()
-            toward(p, lambda step: part_z(p, n, step).wait_send())
+            toward(p, lambda step: both_sent(part_z(p, n, step, False), part_z(p, n, step, True)))
 
     for n in range(chunks):
         part_b(n).wait_send()
@@ -301,7 +339,7 @@
     row_b = rows * B_SHARE // 8
     row_a = rows - row_b
     kept = row_a + 2 * row_b
-    chunks = 4
+    chunks = 2
     wide = width // chunks
     core = lax.axis_index("grp")
     ids = lax.rem(core + jnp.arange(8, dtype=jnp.int32), 2)[None, :] * members + jnp.arange(members, dtype=jnp.int32)[:, None]
@@ -324,14 +362,17 @@
             pltpu.VMEM((planes, chunks, kept, wide), jnp.float32),
             pltpu.VMEM((planes, chunks, row_a, wide), bf),
             pltpu.VMEM((planes, chunks, row_a, wide), bf),
-            pltpu.VMEM((planes, chunks, kept, wide), bf),
-            pltpu.VMEM((planes + 1, chunks, kept, wide), bf),
+            pltpu.VMEM((planes, chunks, row_a, wide), bf),
+            pltpu.VMEM((planes, chunks, 2 * row_b, wide), bf),
+            pltpu.VMEM((planes + 1, chunks, row_a, wide), bf),
+            pltpu.VMEM((planes + 1, chunks, 2 * row_b, wide), bf),
             pltpu.VMEM((chunks, row_b, wide), bf),
             pltpu.VMEM((chunks, row_b, wide), bf),
-            dma((4,)), dma((3,)), dma((3,)), dma((members,)), dma((members,)),
+            dma((5,)), dma((3,)), dma((3,)), dma((members,)), dma((members,)),
             dma((planes + 1,)), dma((planes + 1,)), dma((planes,)), dma((planes,)),
             dma((planes,)), dma((planes,)), dma((1,)), dma((1,)),
             dma((planes, chunks)), dma((planes, chunks)), dma((planes, chunks)), dma((planes + 1, chunks)),
+            dma((planes, chunks)), dma((planes + 1, chunks)),
             dma((chunks,)), dma((chunks,)),
         ],
         compiler_params=pltpu.CompilerParams(collective_id=0, has_side_effects=True, vmem_limit_bytes=60 * 1024 * 1024),

time: 118 us -> 111 us (0.941)
  Pallas kernels: 115 us -> 107 us
    pallas_call x1, Pallas kernels: 115 us -> 107 us  [fused(): pl.pallas_call(mixing_kernel, out_shape=jax.ShapeDtypeStruct((rows, width...]
where the time goes in v3:
time: 111 us
  Pallas kernels  107 us (96%)
  local copies, waits for them, and re-layouts  1.88 us (2%)
  other arithmetic  1.43 us (1%)
    pallas_call x1, Pallas kernels, fused(): pl.pallas_call(mixing_kernel, out_shape=jax.ShapeDtypeStruct((rows, width...  107 us

profile of v3, /device:TPU:0, one launch (start us, length us, event | category | flops | bytes accessed | tf_op | source)
XLA Modules:
  0.0 110.7 jit_solution(3000509104203713486)
XLA Ops:
  0.0 1.4 %select_reduce_fusion.shares_ref = f32[8,8,128]{2,1,0:T(8,128)} fusion(f32[8,128]{1,0:T(8,128)} %bitcast.2, s32[8,8]{1,0:T(8,128)S(1)} %iota_add_fusion, s32[8,128]{1,0:T(8,128)} %bitcast.3), kind=kLoop, calls=%fused_computation | loop fusion | flops 188416 | bytes 41216 | tf_op jit(solution)/shard_map/reduce_sum | solution.py:346
  1.4 107.4 %shard_map.64 = bf16[128,2048]{1,0:T(8,128)(2,1)} custom-call(bf16[128,2048]{1,0:T(8,128)(2,1)} %tokens_ref.1, f32[8,8,128]{2,1,0:T(8,128)} %select_reduce_fusion.shares_ref, bf16[1,2048,768]{2,1,0:T(8,128)(2,1)} %wg_hbm.1, bf16[1,2048,768]{2,1,0:T(8,128)(2,1)} %wu_hbm.1, bf16[1,768,2048]{2,1,0:T(8,128)(2,1)} %wd_hbm.1), custom_call_target="tpu_custom_call" | custom-call | flops 19327352832 | bytes 20971520 | tf_op jit(solution)/shard_map/pallas_call | solution.py:349
  108.8 1.9 %copy.8 = bf16[128,2048]{1,0:T(8,128)(2,1)} copy(bf16[128,2048]{1,0:T(8,128)(2,1)} %shard_map.64) | data formatting | bytes 1048576
  (2 shorter events, 0.0 us)

commit v4 on v3

--- a/solution.py
+++ b/solution.py
@@ -174,7 +174,7 @@
             scale[e, rng_mb, :] = mine[row_a:]
             scale[e, rng_ob, :] = other[row_a:]
 
-    tile = 256
+    tile = 768
 
     def make_hidden(p, e, part):
         @pl.loop(0, hidden // tile)

time: 111 us -> 108 us (0.973)
  Pallas kernels: 107 us -> 104 us
    pallas_call x1, Pallas kernels: 107 us -> 104 us  [fused(): pl.pallas_call(mixing_kernel, out_shape=jax.ShapeDtypeStruct((rows, width...]
where the time goes in v4:
time: 108 us
  Pallas kernels  104 us (96%)
  local copies, waits for them, and re-layouts  1.88 us (2%)
  other arithmetic  1.43 us (1%)
    pallas_call x1, Pallas kernels, fused(): pl.pallas_call(mixing_kernel, out_shape=jax.ShapeDtypeStruct((rows, width...  104 us

profile of v4, /device:TPU:0, one launch (start us, length us, event | category | flops | bytes accessed | tf_op | source)
XLA Modules:
  0.0 107.5 jit_solution(10847869550149392508)
XLA Ops:
  0.0 1.4 %select_reduce_fusion.shares_ref = f32[8,8,128]{2,1,0:T(8,128)} fusion(f32[8,128]{1,0:T(8,128)} %bitcast.2, s32[8,8]{1,0:T(8,128)S(1)} %iota_add_fusion, s32[8,128]{1,0:T(8,128)} %bitcast.3), kind=kLoop, calls=%fused_computation | loop fusion | flops 188416 | bytes 41216 | tf_op jit(solution)/shard_map/reduce_sum | solution.py:346
  1.4 104.2 %shard_map.64 = bf16[128,2048]{1,0:T(8,128)(2,1)} custom-call(bf16[128,2048]{1,0:T(8,128)(2,1)} %tokens_ref.1, f32[8,8,128]{2,1,0:T(8,128)} %select_reduce_fusion.shares_ref, bf16[1,2048,768]{2,1,0:T(8,128)(2,1)} %wg_hbm.1, bf16[1,2048,768]{2,1,0:T(8,128)(2,1)} %wu_hbm.1, bf16[1,768,2048]{2,1,0:T(8,128)(2,1)} %wd_hbm.1), custom_call_target="tpu_custom_call" | custom-call | flops 19327352832 | bytes 20971520 | tf_op jit(solution)/shard_map/pallas_call | solution.py:349
  105.6 1.9 %copy.8 = bf16[128,2048]{1,0:T(8,128)(2,1)} copy(bf16[128,2048]{1,0:T(8,128)(2,1)} %shard_map.64) | data formatting | bytes 1048576
  (2 shorter events, 0.0 us)
